TPU v7x, 256 devices: a whole 4x4x8 slice. The times are simulated.
256 devices in a mesh: grp: 32 (over x, y, core), blk: 8 (over z).
Axes of the slice: x: 4, y: 4, z: 8, core: 2. Of those that a mesh axis runs over, the one named last changes fastest.
Arguments:
- tiles_near: bfloat16 [16384, 256, 256], P(('grp', 'blk')), may hold values from -0.078125 to 0.078125
- near_cols: int32 [256, 64], P(('grp', 'blk')), may hold values from 0 to 3
- tiles_far: bfloat16 [6144, 256, 256], P(('grp', 'blk')), may hold values from -0.078125 to 0.078125
- far_groups: int32 [256, 24], P(('grp', 'blk')), may hold values from 0 to 31, as said below
- need_blocks: int32 [256, 32], P(('grp', 'blk')), may hold values from -1 to 3, as said below
- start_vectors: bfloat16 [262144, 128], P(('grp', 'blk')), may hold values from -6 to 6
Outputs:
- vectors: float32 [262144, 128], P(('grp', 'blk'))
Inputs may be any that keep to these rules, and one draw needn't show every extreme that they name: need_blocks[d, h] is -1 for d's own group and for groups d reads nothing from, else a row block index below 4 of the device of group h at d's position along blk; every device reads from at least one other group. far_groups[d, t] is a group h with need_blocks[d, h] >= 0.
All inputs are finite; a program needn't handle non-finite values.
Results may differ from a plain program's by a relative error of at most 0.0029.
Values may be sent and summed in bfloat16 or wider, within the bound.
A program may use at most 128 MiB of HBM per device.

v0:
```python
import jax
import jax.numpy as jnp
from jax import lax
from jax.sharding import PartitionSpec as P

ITERS = 2


def per_device(tiles_near, near_cols, tiles_far, far_groups, need_blocks, start_vectors):
    tile_size = tiles_near.shape[1]
    vec_width = start_vectors.shape[1]
    blocks = start_vectors.shape[0] // tile_size
    group_size = lax.axis_size("blk")
    group_count = lax.axis_size("grp")
    per_source = tiles_near.shape[0] // (blocks * group_size)
    far_each = tiles_far.shape[0] // blocks
    near_tiles = tiles_near.reshape(blocks, group_size, per_source, tile_size, tile_size)
    near_index = near_cols.reshape(blocks, group_size, per_source)
    far_tiles = tiles_far.reshape(blocks, far_each, tile_size, tile_size)
    far_index = far_groups.reshape(blocks, far_each)
    wanted = need_blocks.reshape(group_count)
    total_rows = blocks * tile_size * group_size * group_count
    current = start_vectors
    vectors = start_vectors.astype(jnp.float32)
    for iteration in range(ITERS):
        local_rows = current.reshape(blocks, tile_size, vec_width)
        group_table = lax.all_gather(local_rows, "blk", axis=0, tiled=True)
        source_ids = jnp.arange(group_size, dtype=jnp.int32)[None, :, None]
        chosen = group_table[source_ids * blocks + near_index]
        near_part = jnp.einsum(
            "rmnij,rmnjk->rik", near_tiles, chosen, preferred_element_type=jnp.float32
        )
        everything = lax.all_gather(local_rows, "grp", axis=0, tiled=True)
        far_rows = everything[far_index * blocks + wanted[far_index]]
        far_part = jnp.einsum(
            "rnij,rnjk->rik", far_tiles, far_rows, preferred_element_type=jnp.float32
        )
        product = near_part + far_part
        flat_rows = product.reshape(blocks * tile_size, vec_width)
        local_gram = jnp.dot(
            flat_rows.T,
            flat_rows,
            precision=lax.Precision.HIGHEST,
            preferred_element_type=jnp.float32,
        )
        gram = lax.psum(local_gram, ("grp", "blk")) / total_rows
        factor = jnp.linalg.cholesky(gram)
        identity_matrix = jnp.eye(vec_width, dtype=jnp.float32)
        inverse = lax.linalg.triangular_solve(factor, identity_matrix, left_side=True, lower=True).T
        vectors = jnp.dot(
            flat_rows, inverse, precision=lax.Precision.HIGHEST, preferred_element_type=jnp.float32
        )
        current = vectors.astype(jnp.bfloat16)
    return vectors


def solution(mesh):
    in_specs = (
        P(("grp", "blk"), None, None),
        P(("grp", "blk"), None),
        P(("grp", "blk"), None, None),
        P(("grp", "blk"), None),
        P(("grp", "blk"), None),
        P(("grp", "blk"), None),
    )
    out_specs = P(("grp", "blk"), None)
    return jax.shard_map(
        per_device, mesh=mesh, in_specs=in_specs, out_specs=out_specs, check_vma=False
    )
```

profile of v0, /device:TPU:1, one launch (start us, length us, event | category | flops | bytes accessed | tf_op | source)
XLA Modules:
  0.0 777.3 jit_solution(7489281376360508679)
XLA Ops:
  10.1 1.4 gather_fusion.1
  11.6 1.3 reduce.11
  13.3 37.1 %all-gather.5.cloned.1.call-done = bf16[32,256,128]{2,1,0:T(8,128)(2,1)} async-done(((bf16[4,256,128]{2,1,0:T(8,128)(2,1)}), bf16[32,256,128]{2,1,0:T(8,128)(2,1)}) %all-gather.5.cloned.1.call-update) | async-done | bytes 2097168 | tf_op jit(solution)/shard_map/all_gather | solution.py:27
  50.4 4.6 gather_fusion
  55.0 58.5 %all-gather.7.cloned.1.call-done = bf16[128,256,128]{2,1,0:T(8,128)(2,1)} async-done(((bf16[4,256,128]{2,1,0:T(8,128)(2,1)}), bf16[128,256,128]{2,1,0:T(8,128)(2,1)}) %all-gather.7.cloned.1.call-update) | async-done | bytes 8388624 | tf_op jit(solution)/shard_map/all_gather | solution.py:33
  113.6 5.4 gather_fusion.2
  118.9 2.7 convolution_bitcast_fusion.1
  121.7 5.2 fusion.31
  129.0 2.0 copy.32
  131.0 235.3 %all-reduce.3.cloned.1.call-done = f32[128,128]{0,1:T(8,128)} async-done(((f32[128,128]{0,1:T(8,128)}), f32[128,128]{0,1:T(8,128)}) %all-reduce.3.cloned.1.call-update) | async-done | bytes 65552 | tf_op jit(solution)/shard_map/psum | solution.py:46
  368.1 11.7 %cholesky.44 = f32[128,128]{1,0:T(8,128)S(1)} custom-call(f32[128,128]{1,0:T(8,128)S(1)} %fusion.45), custom_call_target="Cholesky" | custom-call | tf_op jit(solution)/shard_map/jit(cholesky)/cholesky | solution.py:47
  381.2 9.8 %custom-call.6 = f32[1,128,128]{1,2,0:T(8,128)S(1)} custom-call(f32[1,128,128]{2,1,0:T(8,128)S(1)} %fusion.40), custom_call_target="InvertDiagBlocksLowerTriangular" | custom-call | tf_op jit(solution)/shard_map/triangular_solve/custom-call.0 | solution.py:49
  391.3 2.3 convolution_convert_fusion
  394.5 32.8 %all-gather.9.cloned.1.call-done = bf16[32,256,128]{2,1,0:T(8,128)(2,1)} async-done(((bf16[4,256,128]{2,1,0:T(8,128)(2,1)}), bf16[32,256,128]{2,1,0:T(8,128)(2,1)}) %all-gather.9.cloned.1.call-update) | async-done | bytes 2097168 | tf_op jit(solution)/shard_map/all_gather | solution.py:27
  427.3 4.6 gather_fusion.3
  432.0 58.4 %all-gather.11.cloned.1.call-done = bf16[128,256,128]{2,1,0:T(8,128)(2,1)} async-done(((bf16[4,256,128]{2,1,0:T(8,128)(2,1)}), bf16[128,256,128]{2,1,0:T(8,128)(2,1)}) %all-gather.11.cloned.1.call-update) | async-done | bytes 8388624 | tf_op jit(solution)/shard_map/all_gather | solution.py:33
  490.3 5.4 gather_fusion.4
  495.7 2.7 convolution_bitcast_fusion
  498.4 5.2 fusion.21
  505.7 2.0 copy.39
  507.7 235.3 %all-reduce.5.cloned.1.call-done = f32[128,128]{0,1:T(8,128)} async-done(((f32[128,128]{0,1:T(8,128)}), f32[128,128]{0,1:T(8,128)}) %all-reduce.5.cloned.1.call-update) | async-done | bytes 65552 | tf_op jit(solution)/shard_map/psum | solution.py:46
  744.9 11.7 %cholesky.55 = f32[128,128]{1,0:T(8,128)S(1)} custom-call(f32[128,128]{1,0:T(8,128)S(1)} %fusion.43), custom_call_target="Cholesky" | custom-call | tf_op jit(solution)/shard_map/jit(cholesky)/cholesky | solution.py:47
  757.9 9.8 %custom-call.7 = f32[1,128,128]{1,2,0:T(8,128)S(1)} custom-call(f32[1,128,128]{2,1,0:T(8,128)S(1)} %fusion.41), custom_call_target="InvertDiagBlocksLowerTriangular" | custom-call | tf_op jit(solution)/shard_map/triangular_solve/custom-call.0 | solution.py:49
  768.0 2.4 fusion.46
  (53 shorter events, 15.7 us)
Async XLA Ops:
  6.5 112.4 %copy-start = (bf16[24,256,256]{2,1,0:T(8,128)(2,1)S(1)}, bf16[24,256,256]{2,1,0:T(8,128)(2,1)}, u32[]{:S(2)}) copy-start(bf16[24,256,256]{2,1,0:T(8,128)(2,1)} %param.11) | copy-start | bytes 9437188
  6.5 43.8 %all-gather.5.cloned.1.call-start = ((), (), s32[]{:S(2)}) async-start(), calls=%async_computation | async-start | bytes 2359296 | tf_op jit(solution)/shard_map/all_gather | solution.py:27
  7.3 106.3 %all-gather.7.cloned.1.call-start = ((), (), s32[]{:S(2)}) async-start(), calls=%async_computation.1 | async-start | bytes 8650752 | tf_op jit(solution)/shard_map/all_gather | solution.py:33
  8.0 358.3 %all-reduce.3.cloned.1.call-start = ((), (), s32[]{:S(2)}) async-start(), calls=%async_computation.2 | async-start | bytes 131072 | tf_op jit(solution)/shard_map/psum | solution.py:46
  118.9 2.7 copy-start.4
  126.9 0.8 copy-start.1
  128.9 298.4 %all-gather.9.cloned.1.call-start = ((), (), s32[]{:S(2)}) async-start(), calls=%async_computation.3 | async-start | bytes 2359296 | tf_op jit(solution)/shard_map/all_gather | solution.py:27
  393.6 96.7 %all-gather.11.cloned.1.call-start = ((), (), s32[]{:S(2)}) async-start(), calls=%async_computation.4 | async-start | bytes 8650752 | tf_op jit(solution)/shard_map/all_gather | solution.py:33
  394.2 348.8 %all-reduce.5.cloned.1.call-start = ((), (), s32[]{:S(2)}) async-start(), calls=%async_computation.5 | async-start | bytes 131072 | tf_op jit(solution)/shard_map/psum | solution.py:46
  495.7 2.7 copy-start.3
  503.7 0.8 copy-start.2
Sparse Core Ops, SparseCore 0:
  9.1 41.1 all-gather.4
  52.9 60.5 all-gather.6
  129.1 237.2 all-reduce.2
  393.8 33.4 all-gather.8
  429.7 60.5 all-gather.10
  505.8 237.1 all-reduce.4
where the time goes:
time: 778 us; the launch traced here: 777 us
  waiting for transfers between devices  659 us (85%)
  other arithmetic  51.9 us (7%)
  local copies, waits for them, and re-layouts  28.3 us (4%)
  matrix products  23.6 us (3%)
  between operations  13.7 us (2%)
    psum x2, waiting for transfers between devices, per_device(): gram = lax.psum(local_gram, ('grp', 'blk')) / total_rows  471 us
    all_gather x2, waiting for transfers between devices, per_device(): everything = lax.all_gather(local_rows, 'grp', axis=0, tiled=True)  117 us
    all_gather x2, waiting for transfers between devices, per_device(): group_table = lax.all_gather(local_rows, 'blk', axis=0, tiled=True)  70 us
    another operation x6, other arithmetic, per_device(): factor = jnp.linalg.cholesky(gram)  24.8 us
    another operation x4, other arithmetic, per_device(): lax.linalg.triangular_solve(factor, identity_matrix, left_side=True, lowe...  20.9 us
  transfers between devices with their start and end apart: 6, of which 6 were waited for; matrix products, arithmetic and copies ran while one was open for 2% of the time, Pallas kernels for 0%

commit v1 on v0

--- a/solution.py
+++ b/solution.py
@@ -4,6 +4,10 @@
 from jax.sharding import PartitionSpec as P
 
 ITERS = 2
+
+
+def cut_things_here(piece_in):
+    return jnp.sum(jax.lax.all_gather(piece_in, axis_name=("grp", "blk")), axis=0)
 
 
 def per_device(tiles_near, near_cols, tiles_far, far_groups, need_blocks, start_vectors):
@@ -43,7 +47,7 @@
             precision=lax.Precision.HIGHEST,
             preferred_element_type=jnp.float32,
         )
-        gram = lax.psum(local_gram, ("grp", "blk")) / total_rows
+        gram = cut_things_here(local_gram) / total_rows
         factor = jnp.linalg.cholesky(gram)
         identity_matrix = jnp.eye(vec_width, dtype=jnp.float32)
         inverse = lax.linalg.triangular_solve(factor, identity_matrix, left_side=True, lower=True).T

time: 778 us -> 563 us (0.72)
  waiting for transfers between devices: 659 us -> 435 us
  other arithmetic: 51.9 us -> 61.7 us
    psum x2 -> x0, waiting for transfers between devices: 471 us -> none  [per_device(): gram = lax.psum(local_gram, ('grp', 'blk')) / total_rows]
    all_gather x0 -> x2, waiting for transfers between devices: none -> 245 us  [cut_things_here(): jax.lax.all_gather(piece_in, axis_name=('grp', 'blk'))]
    reduce_sum x0 -> x2, other arithmetic: none -> 13.2 us  [cut_things_here(): jnp.sum(jax.lax.all_gather(piece_in, axis_name=('grp', 'blk')), axis=0)]
  transfers between devices with their start and end apart: 6 -> 6, of which waited for: 6 -> 6; matrix products, arithmetic and copies ran while one was open for 2% -> 3% of each run, Pallas kernels for 0% -> 0%
where the time goes in v1:
time: 563 us
  waiting for transfers between devices  435 us (77%)
  other arithmetic  61.7 us (11%)
  local copies, waits for them, and re-layouts  28.5 us (5%)
  matrix products  23.6 us (4%)
  between operations  13.7 us (2%)
    all_gather x2, waiting for transfers between devices, cut_things_here(): jax.lax.all_gather(piece_in, axis_name=('grp', 'blk'))  245 us
    all_gather x2, waiting for transfers between devices, per_device(): everything = lax.all_gather(local_rows, 'grp', axis=0, tiled=True)  117 us
    all_gather x2, waiting for transfers between devices, per_device(): group_table = lax.all_gather(local_rows, 'blk', axis=0, tiled=True)  70.7 us
    another operation x6, other arithmetic, per_device(): factor = jnp.linalg.cholesky(gram)  24.8 us
    another operation x4, other arithmetic, per_device(): lax.linalg.triangular_solve(factor, identity_matrix, left_side=True, lowe...  20.9 us
    reduce_sum x2, other arithmetic, cut_things_here(): jnp.sum(jax.lax.all_gather(piece_in, axis_name=('grp', 'blk')), axis=0)  13.2 us
    gather x4, local copies, waits for them, and re-layouts, per_device(): far_rows = everything[far_index * blocks + wanted[far_index]]  12.2 us
  transfers between devices with their start and end apart: 6, of which 6 were waited for; matrix products, arithmetic and copies ran while one was open for 3% of the time, Pallas kernels for 0%

profile of v1, /device:TPU:1, one launch (start us, length us, event | category | flops | bytes accessed | tf_op | source)
XLA Modules:
  0.0 562.6 jit_solution(3628210382297687145)
XLA Ops:
  13.3 37.1 %all-gather.9.cloned.1.call-done = bf16[32,256,128]{2,1,0:T(8,128)(2,1)} async-done(((bf16[4,256,128]{2,1,0:T(8,128)(2,1)}), bf16[32,256,128]{2,1,0:T(8,128)(2,1)}) %all-gather.9.cloned.1.call-update) | async-done | bytes 2097168 | tf_op jit(solution)/shard_map/all_gather | solution.py:31
  50.4 4.6 gather_fusion
  55.0 58.5 %all-gather.11.cloned.1.call-done = bf16[128,256,128]{2,1,0:T(8,128)(2,1)} async-done(((bf16[4,256,128]{2,1,0:T(8,128)(2,1)}), bf16[128,256,128]{2,1,0:T(8,128)(2,1)}) %all-gather.11.cloned.1.call-update) | async-done | bytes 8388624 | tf_op jit(solution)/shard_map/all_gather | solution.py:37
  113.6 5.4 gather_fusion.2
  118.9 2.7 convolution_bitcast_fusion.1
  121.7 5.2 fusion.31
  129.0 2.0 copy.28
  131.0 122.5 %all-gather.17.cloned.1.call-done = f32[32768,128]{1,0:T(8,128)} async-done(((f32[128,128]{1,0:T(8,128)}), f32[32768,128]{1,0:T(8,128)}) %all-gather.17.cloned.1.call-update) | async-done | bytes 16777232 | tf_op jit(solution)/shard_map/all_gather | solution.py:10
  253.6 6.6 %reduce_sum.18 = f32[128,128]{1,0:T(8,128)S(1)} reduce(f32[256,128,128]{2,1,0:T(8,128)} %bitcast.84, f32[]{:T(128)} %constant.44.clone.1), dimensions={0}, to_apply=%region_0.0 | reduce | flops 4177920 | bytes 16842756 | tf_op jit(solution)/shard_map/reduce_sum | solution.py:10
  260.4 11.7 %cholesky.44 = f32[128,128]{1,0:T(8,128)S(1)} custom-call(f32[128,128]{1,0:T(8,128)S(1)} %fusion.45), custom_call_target="Cholesky" | custom-call | tf_op jit(solution)/shard_map/jit(cholesky)/cholesky | solution.py:51
  273.4 9.8 %custom-call.6 = f32[1,128,128]{1,2,0:T(8,128)S(1)} custom-call(f32[1,128,128]{2,1,0:T(8,128)S(1)} %fusion.40), custom_call_target="InvertDiagBlocksLowerTriangular" | custom-call | tf_op jit(solution)/shard_map/triangular_solve/custom-call.0 | solution.py:53
  283.5 2.3 convolution_convert_fusion
  286.7 33.6 %all-gather.13.cloned.1.call-done = bf16[32,256,128]{2,1,0:T(8,128)(2,1)} async-done(((bf16[4,256,128]{2,1,0:T(8,128)(2,1)}), bf16[32,256,128]{2,1,0:T(8,128)(2,1)}) %all-gather.13.cloned.1.call-update) | async-done | bytes 2097168 | tf_op jit(solution)/shard_map/all_gather | solution.py:31
  320.3 4.6 gather_fusion.3
  325.0 58.4 %all-gather.15.cloned.1.call-done = bf16[128,256,128]{2,1,0:T(8,128)(2,1)} async-done(((bf16[4,256,128]{2,1,0:T(8,128)(2,1)}), bf16[128,256,128]{2,1,0:T(8,128)(2,1)}) %all-gather.15.cloned.1.call-update) | async-done | bytes 8388624 | tf_op jit(solution)/shard_map/all_gather | solution.py:37
  383.3 5.4 gather_fusion.4
  388.7 2.7 convolution_bitcast_fusion
  391.5 5.2 fusion.21
  398.7 2.0 copy.35
  400.8 122.6 %all-gather.19.cloned.1.call-done = f32[32768,128]{1,0:T(8,128)} async-done(((f32[128,128]{1,0:T(8,128)}), f32[32768,128]{1,0:T(8,128)}) %all-gather.19.cloned.1.call-update) | async-done | bytes 16777232 | tf_op jit(solution)/shard_map/all_gather | solution.py:10
  523.4 6.6 %reduce_sum.19 = f32[128,128]{1,0:T(8,128)S(1)} reduce(f32[256,128,128]{2,1,0:T(8,128)} %bitcast.85, f32[]{:T(128)} %constant.44.clone.1), dimensions={0}, to_apply=%region_3.6 | reduce | flops 4177920 | bytes 16842756 | tf_op jit(solution)/shard_map/reduce_sum | solution.py:10
  530.2 11.7 %cholesky.55 = f32[128,128]{1,0:T(8,128)S(1)} custom-call(f32[128,128]{1,0:T(8,128)S(1)} %fusion.43), custom_call_target="Cholesky" | custom-call | tf_op jit(solution)/shard_map/jit(cholesky)/cholesky | solution.py:51
  543.2 9.8 %custom-call.7 = f32[1,128,128]{1,2,0:T(8,128)S(1)} custom-call(f32[1,128,128]{2,1,0:T(8,128)S(1)} %fusion.41), custom_call_target="InvertDiagBlocksLowerTriangular" | custom-call | tf_op jit(solution)/shard_map/triangular_solve/custom-call.0 | solution.py:53
  553.3 2.4 fusion.46
  (57 shorter events, 15.1 us)
Async XLA Ops:
  6.5 112.4 %copy-start = (bf16[24,256,256]{2,1,0:T(8,128)(2,1)S(1)}, bf16[24,256,256]{2,1,0:T(8,128)(2,1)}, u32[]{:S(2)}) copy-start(bf16[24,256,256]{2,1,0:T(8,128)(2,1)} %param.11) | copy-start | bytes 9437188
  6.5 43.8 %all-gather.9.cloned.1.call-start = ((), (), s32[]{:S(2)}) async-start(), calls=%async_computation | async-start | bytes 2359296 | tf_op jit(solution)/shard_map/all_gather | solution.py:31
  7.3 106.3 %all-gather.11.cloned.1.call-start = ((), (), s32[]{:S(2)}) async-start(), calls=%async_computation.1 | async-start | bytes 8650752 | tf_op jit(solution)/shard_map/all_gather | solution.py:37
  8.0 245.6 %all-gather.17.cloned.1.call-start = ((), (), s32[]{:S(2)}) async-start(), calls=%async_computation.4 | async-start | bytes 16842752 | tf_op jit(solution)/shard_map/all_gather | solution.py:10
  118.9 2.7 copy-start.4
  126.9 0.8 copy-start.1
  128.9 191.4 %all-gather.13.cloned.1.call-start = ((), (), s32[]{:S(2)}) async-start(), calls=%async_computation.2 | async-start | bytes 2359296 | tf_op jit(solution)/shard_map/all_gather | solution.py:31
  285.9 97.4 %all-gather.15.cloned.1.call-start = ((), (), s32[]{:S(2)}) async-start(), calls=%async_computation.3 | async-start | bytes 8650752 | tf_op jit(solution)/shard_map/all_gather | solution.py:37
  286.5 236.9 %all-gather.19.cloned.1.call-start = ((), (), s32[]{:S(2)}) async-start(), calls=%async_computation.5 | async-start | bytes 16842752 | tf_op jit(solution)/shard_map/all_gather | solution.py:10
  388.7 2.7 copy-start.3
  396.7 0.8 copy-start.2
Sparse Core Ops, SparseCore 0:
  9.1 41.1 all-gather.8
  52.9 60.5 all-gather.10
  129.1 124.4 all-gather.16
  286.0 34.2 all-gather.12
  322.7 60.5 all-gather.14
  398.8 124.4 all-gather.18
